TPU v7x, 32 devices: a whole 2x2x4 slice. The times are simulated.
32 devices in a mesh: date: 2 (over y), row: 16 (over z, x, core).
Axes of the slice: x: 2, y: 2, z: 4, core: 2. Of those that a mesh axis runs over, the one named last changes fastest.
Arguments:
- slc: float32 [2, 128, 128, 256], P(None, 'date', 'row'), may hold values from -40 to 40, as said below
- network: int32 [128, 8], replicated, may hold values 0 or 1
Outputs:
- linked: float32 [2, 128, 128, 256], P(None, None, 'row', 'date')
Inputs may be any that keep to these rules, and one draw needn't show every extreme that they name: slc holds real and imaginary parts of complex samples.
All inputs are finite; a program needn't handle non-finite values.
Results may differ from a plain program's by a relative error of at most 0.0003.
Values sent between devices are 32-bit elements; how exact they have to be, the bound alone decides.
A program may use at most 192 MiB of HBM per device.

v0:
```python
import jax
import jax.numpy as jnp
from jax import lax
from jax.sharding import PartitionSpec as P

LOOK = 5
ITERS = 5


def extended_2(cells, sides, width):
    for axis, dim in sides:
        count = lax.axis_size(axis)
        ends = count - 1
        head = lax.slice_in_dim(cells, 0, width, axis=dim)
        tail = lax.slice_in_dim(cells, cells.shape[dim] - width, cells.shape[dim], axis=dim)
        cells = jnp.concatenate(
            [
                lax.ppermute(tail, axis, [(i, (i + 1) % count) for i in range(ends)]),
                cells,
                lax.ppermute(head, axis, [((i + 1) % count, i) for i in range(ends)]),
            ],
            axis=dim,
        )
    return cells


def band_table(count_out):
    count_in = count_out + 2 * LOOK
    outer = jnp.arange(count_out, dtype=jnp.int32)[:, None]
    inner = jnp.arange(count_in, dtype=jnp.int32)[None, :]
    reach = inner - outer
    return ((reach >= 0) & (reach <= 2 * LOOK)).astype(jnp.float32)


def box_sum(samples):
    rows_out = samples.shape[-2] - 2 * LOOK
    cols_out = samples.shape[-1] - 2 * LOOK
    row_table = band_table(rows_out)
    col_table = band_table(cols_out)
    total = jnp.einsum("...rc,kr->...kc", samples, row_table, precision=lax.Precision.HIGHEST)
    return jnp.einsum("...kc,mc->...km", total, col_table, precision=lax.Precision.HIGHEST)


def coherence(extended, network):
    num_dates = extended.shape[1]
    squares = extended[0] * extended[0] + extended[1] * extended[1]
    inverse_root = lax.rsqrt(box_sum(squares) + 1e-06)
    layers = []
    for offset in range(1, network.shape[1] + 1):
        earlier = extended[:, : num_dates - offset]
        later = extended[:, offset:]
        prod_re = earlier[0] * later[0] + earlier[1] * later[1]
        prod_im = earlier[1] * later[0] - earlier[0] * later[1]
        sums = box_sum(jnp.stack([prod_re, prod_im]))
        weight = network[: num_dates - offset, offset - 1].astype(jnp.float32)[:, None, None]
        weight = weight * inverse_root[: num_dates - offset] * inverse_root[offset:]
        layer = sums * weight[None]
        layers.append(jnp.pad(layer, ((0, 0), (0, offset), (0, 0), (0, 0))))
    return jnp.stack(layers)


def apply_matrix(coherent, vector):
    num_dates = vector.shape[1]
    image_re = vector[0]
    image_im = vector[1]
    for offset in range(1, coherent.shape[0] + 1):
        coh_re = coherent[offset - 1, 0]
        coh_im = coherent[offset - 1, 1]
        ahead = jnp.pad(vector[:, offset:], ((0, 0), (0, offset), (0, 0), (0, 0)))
        image_re = image_re + coh_re * ahead[0] - coh_im * ahead[1]
        image_im = image_im + coh_re * ahead[1] + coh_im * ahead[0]
        back_re = coh_re * vector[0] + coh_im * vector[1]
        back_im = coh_re * vector[1] - coh_im * vector[0]
        image_re = image_re + jnp.pad(back_re[: num_dates - offset], ((offset, 0), (0, 0), (0, 0)))
        image_im = image_im + jnp.pad(back_im[: num_dates - offset], ((offset, 0), (0, 0), (0, 0)))
    image = jnp.stack([image_re, image_im])
    meansq = jnp.mean(image[0] * image[0] + image[1] * image[1], axis=0)
    return image * lax.rsqrt(meansq + 1e-06)[None, None]


def power_iterate(coherent):
    start = jnp.stack([jnp.ones_like(coherent[0, 0]), jnp.zeros_like(coherent[0, 0])])

    def iterate_once(index, vector):
        return apply_matrix(coherent, vector)

    return lax.fori_loop(0, ITERS, iterate_once, start)


def regroup(samples):
    return lax.all_to_all(samples, "date", split_axis=3, concat_axis=1, tiled=True)


def add_row_rims(samples):
    return extended_2(samples, (("row", 2),), LOOK)


def add_column_rims(samples):
    return extended_2(samples, (("date", 3),), LOOK)


def on_device(slc, network):
    extended = add_column_rims(regroup(add_row_rims(slc)))
    coherent = coherence(extended, network)
    return power_iterate(coherent)


def solution(mesh):
    return jax.shard_map(
        on_device,
        mesh=mesh,
        in_specs=(P(None, "date", "row", None), P()),
        out_specs=P(None, None, "row", "date"),
        check_vma=False,
    )
```

profile of v0, /device:TPU:10, one launch (start us, length us, event | category | flops | bytes accessed | tf_op | source)
XLA Modules:
  0.0 409.5 jit_solution(18203681720282301117)
XLA Ops:
  10.9 11.1 %collective-permute-done = f32[2,64,5,256]{3,1,2,0:T(8,128)} collective-permute-done((f32[2,64,5,256]{3,1,2,0:T(8,128)}, f32[2,64,5,256]{3,1,2,0:T(8,128)}, u32[]{:S(2)}, u32[]{:S(2)}) %collective-permute-start) | collective-permute-done | bytes 655392 | tf_op jit(solution)/shard_map/ppermute | solution.py:18
  29.2 6.1 %fusion.153 = f32[256,2,18,64]{3,2,1,0:T(8,128)} fusion(f32[2,64,5,256]{1,2,0,3:T(8,128)} %copy.74, f32[2,64,8,256]{1,2,0,3:T(8,128)S(1)} %copy.73, f32[2,64,5,256]{1,2,0,3:T(8,128)} %copy.72), kind=kLoop, calls=%fused_computation.235 | loop fusion | flops 1179648 | bytes 4718592
  35.2 6.0 %reshape.70 = f32[2,1,294912]{2,1,0:T(1,128)} reshape(f32[256,2,18,64]{3,2,1,0:T(8,128)} %fusion.153) | data formatting | bytes 4718592
  45.6 23.0 %all-to-all-done = f32[2,1,294912]{2,1,0:T(1,128)S(1)} async-done(((f32[2,1,294912]{2,1,0:T(1,128)}), f32[2,1,294912]{2,1,0:T(1,128)S(1)}, u32[]{:S(2)}, u32[]{:S(2)}) %all-to-all-start) | async-done | bytes 2359328 | tf_op jit(solution)/shard_map/all_to_all | solution.py:91
  69.1 9.0 %reduce = f32[2,294912]{1,0:T(2,128)} reduce(f32[2,1,294912]{2,1,0:T(1,128)S(1)} %all-to-all-done, f32[]{:T(128)} %broadcast.224), dimensions={1}, to_apply=%all_to_all.13.reduce_sub_computation | reduce | bytes 4718596 | tf_op jit(solution)/shard_map/all_to_all | solution.py:91
  78.1 7.5 %reshape.71 = f32[256,2,18,64]{3,2,1,0:T(8,128)} reshape(f32[2,294912]{1,0:T(2,128)} %reduce) | data formatting | bytes 4718592
  85.7 6.4 %copy.100 = f32[2,64,18,2,128]{4,3,1,2,0:T(2,128)} copy(f32[2,64,18,2,128]{1,2,0,4,3:T(8,128)} %bitcast.423) | data formatting | bytes 4718592 | tf_op jit(solution)/shard_map/all_to_all | solution.py:91
  113.2 5.5 %multiply_add_fusion.9 = (f32[1,121,18,138]{1,0,3,2:T(1,128)S(1)}, f32[1,121,18,138]{1,0,3,2:T(1,128)S(1)}) fusion(f32[2,128,18,138]{1,0,3,2:T(2,128)S(1)} %pad_maximum_fusion.1), kind=kLoop, calls=%fused_computation.114 | loop fusion | flops 1803384 | bytes 7213536 | tf_op jit(solution)/shard_map/add | solution.py:52
  121.5 6.4 %multiply_add_fusion.8 = (f32[1,120,18,138]{1,0,3,2:T(1,128)}, f32[1,120,18,138]{1,0,3,2:T(1,128)}) fusion(f32[2,128,18,138]{1,0,3,2:T(2,128)S(1)} %pad_maximum_fusion.1), kind=kLoop, calls=%fused_computation.112 | loop fusion | flops 1788480 | bytes 7153920 | tf_op jit(solution)/shard_map/add | solution.py:52
  127.8 6.4 %multiply_add_fusion.11 = (f32[1,123,18,138]{1,0,3,2:T(1,128)}, f32[1,123,18,138]{1,0,3,2:T(1,128)}) fusion(f32[2,128,18,138]{1,0,3,2:T(2,128)S(1)} %pad_maximum_fusion.1), kind=kLoop, calls=%fused_computation.118 | loop fusion | flops 1833192 | bytes 7332768 | tf_op jit(solution)/shard_map/add | solution.py:52
  134.2 6.4 %multiply_add_fusion.10 = (f32[1,122,18,138]{1,0,3,2:T(1,128)}, f32[1,122,18,138]{1,0,3,2:T(1,128)}) fusion(f32[2,128,18,138]{1,0,3,2:T(2,128)S(1)} %pad_maximum_fusion.1), kind=kLoop, calls=%fused_computation.116 | loop fusion | flops 1818288 | bytes 7273152 | tf_op jit(solution)/shard_map/add | solution.py:52
  140.6 6.6 %multiply_add_fusion.13 = (f32[1,125,18,138]{1,0,3,2:T(1,128)}, f32[1,125,18,138]{1,0,3,2:T(1,128)}) fusion(f32[2,128,18,138]{1,0,3,2:T(2,128)S(1)} %pad_maximum_fusion.1), kind=kLoop, calls=%fused_computation.122 | loop fusion | flops 1863000 | bytes 7452000 | tf_op jit(solution)/shard_map/add | solution.py:52
  147.2 6.4 %multiply_add_fusion.12 = (f32[1,124,18,138]{1,0,3,2:T(1,128)}, f32[1,124,18,138]{1,0,3,2:T(1,128)}) fusion(f32[2,128,18,138]{1,0,3,2:T(2,128)S(1)} %pad_maximum_fusion.1), kind=kLoop, calls=%fused_computation.120 | loop fusion | flops 1848096 | bytes 7392384 | tf_op jit(solution)/shard_map/add | solution.py:52
  153.6 6.5 %multiply_add_fusion.15 = (f32[1,127,18,138]{1,0,3,2:T(1,128)}, f32[1,127,18,138]{1,0,3,2:T(1,128)}) fusion(f32[2,128,18,138]{1,0,3,2:T(2,128)S(1)} %pad_maximum_fusion.1), kind=kLoop, calls=%fused_computation.126 | loop fusion | flops 1892808 | bytes 7571232 | tf_op jit(solution)/shard_map/add | solution.py:52
  160.1 6.4 %multiply_add_fusion.14 = (f32[1,126,18,138]{1,0,3,2:T(1,128)}, f32[1,126,18,138]{1,0,3,2:T(1,128)}) fusion(f32[2,128,18,138]{1,0,3,2:T(2,128)S(1)} %pad_maximum_fusion.1), kind=kLoop, calls=%fused_computation.124 | loop fusion | flops 1877904 | bytes 7511616 | tf_op jit(solution)/shard_map/add | solution.py:52
  169.3 6.7 %copy.94 = f32[2,121,18,138]{3,2,1,0:T(8,128)} copy(f32[2,121,18,138]{1,0,3,2:T(2,128)S(1)} %pad_maximum_fusion.8) | data formatting | bytes 4809024 | tf_op jit(solution)/shard_map/stack | solution.py:54
  176.0 6.2 %fusion.91 = f32[8,2,121,138]{3,0,2,1:T(8,128)} fusion(f32[2,121,18,138]{3,2,1,0:T(8,128)} %copy.94), kind=kOutput, calls=%fused_computation.174 | convolution fusion | flops 57708864 | bytes 3473184 | tf_op jit(solution)/shard_map/...rc,kr->...kc/dot_general | solution.py:40
  188.1 6.3 %copy.96 = f32[2,120,18,138]{3,2,1,0:T(8,128)} copy(f32[2,120,18,138]{1,0,3,2:T(2,128)S(1)} %pad_maximum_fusion.9) | data formatting | bytes 4769280 | tf_op jit(solution)/shard_map/stack | solution.py:54
  194.4 6.1 %fusion.89 = f32[8,2,120,138]{3,0,2,1:T(8,128)} fusion(f32[2,120,18,138]{3,2,1,0:T(8,128)} %copy.96), kind=kOutput, calls=%fused_computation.172 | convolution fusion | flops 57231936 | bytes 3444480 | tf_op jit(solution)/shard_map/...rc,kr->...kc/dot_general | solution.py:40
  204.7 6.3 %copy.90 = f32[2,123,18,138]{3,2,1,0:T(8,128)} copy(f32[2,123,18,138]{1,0,3,2:T(2,128)S(1)} %pad_maximum_fusion.6) | data formatting | bytes 4888512 | tf_op jit(solution)/shard_map/stack | solution.py:54
  211.0 6.1 %fusion.95 = f32[8,2,123,138]{3,0,2,1:T(8,128)} fusion(f32[2,123,18,138]{3,2,1,0:T(8,128)} %copy.90), kind=kOutput, calls=%fused_computation.178 | convolution fusion | flops 58662720 | bytes 3530592 | tf_op jit(solution)/shard_map/...rc,kr->...kc/dot_general | solution.py:40
  221.8 6.5 %copy.92 = f32[2,122,18,138]{3,2,1,0:T(8,128)} copy(f32[2,122,18,138]{1,0,3,2:T(2,128)S(1)} %pad_maximum_fusion.7) | data formatting | bytes 4848768 | tf_op jit(solution)/shard_map/stack | solution.py:54
  228.3 6.0 %fusion.93 = f32[8,2,122,138]{3,0,2,1:T(8,128)} fusion(f32[2,122,18,138]{3,2,1,0:T(8,128)} %copy.92), kind=kOutput, calls=%fused_computation.176 | convolution fusion | flops 58185792 | bytes 3501888 | tf_op jit(solution)/shard_map/...rc,kr->...kc/dot_general | solution.py:40
  239.0 6.3 %copy.86 = f32[2,125,18,138]{3,2,1,0:T(8,128)} copy(f32[2,125,18,138]{1,0,3,2:T(2,128)S(1)} %pad_maximum_fusion.4) | data formatting | bytes 4968000 | tf_op jit(solution)/shard_map/stack | solution.py:54
  245.3 6.2 %fusion.99 = f32[8,2,125,138]{3,0,2,1:T(8,128)} fusion(f32[2,125,18,138]{3,2,1,0:T(8,128)} %copy.86), kind=kOutput, calls=%fused_computation.182 | convolution fusion | flops 59616576 | bytes 3588000 | tf_op jit(solution)/shard_map/...rc,kr->...kc/dot_general | solution.py:40
  256.2 6.8 %copy.88 = f32[2,124,18,138]{3,2,1,0:T(8,128)} copy(f32[2,124,18,138]{1,0,3,2:T(2,128)S(1)} %pad_maximum_fusion.5) | data formatting | bytes 4928256 | tf_op jit(solution)/shard_map/stack | solution.py:54
  263.0 6.2 %fusion.97 = f32[8,2,124,138]{3,0,2,1:T(8,128)} fusion(f32[2,124,18,138]{3,2,1,0:T(8,128)} %copy.88), kind=kOutput, calls=%fused_computation.180 | convolution fusion | flops 59139648 | bytes 3559296 | tf_op jit(solution)/shard_map/...rc,kr->...kc/dot_general | solution.py:40
  273.9 6.3 %copy.80 = f32[2,127,18,138]{3,2,1,0:T(8,128)} copy(f32[2,127,18,138]{1,0,3,2:T(2,128)S(1)} %pad_maximum_fusion.2) | data formatting | bytes 5047488 | tf_op jit(solution)/shard_map/stack | solution.py:54
  280.2 6.3 %fusion.103 = f32[8,2,127,138]{3,0,2,1:T(8,128)} fusion(f32[2,127,18,138]{3,2,1,0:T(8,128)} %copy.80), kind=kOutput, calls=%fused_computation.186 | convolution fusion | flops 60570432 | bytes 3645408 | tf_op jit(solution)/shard_map/...rc,kr->...kc/dot_general | solution.py:40
  291.3 6.5 %copy.84 = f32[2,126,18,138]{3,2,1,0:T(8,128)} copy(f32[2,126,18,138]{1,0,3,2:T(2,128)S(1)} %pad_maximum_fusion.3) | data formatting | bytes 5007744 | tf_op jit(solution)/shard_map/stack | solution.py:54
  297.7 4.9 %fusion.101 = f32[8,2,126,138]{3,0,2,1:T(8,128)S(1)} fusion(f32[2,126,18,138]{3,2,1,0:T(8,128)} %copy.84), kind=kOutput, calls=%fused_computation.184 | convolution fusion | flops 60093504 | bytes 3616704 | tf_op jit(solution)/shard_map/...rc,kr->...kc/dot_general | solution.py:40
  322.6 85.7 %while.12 = (s32[]{:T(128)}, f32[2,128,8,128]{3,2,1,0:T(8,128)S(1)}, f32[1,2,128,8,128]{4,3,2,1,0:T(8,128)}, f32[1,2,128,8,128]{4,3,2,1,0:T(8,128)}, f32[1,2,128...) while((s32[]{:T(128)}, ...), condition=%wide.region_2.3_spmd, body=%wide.region_0.2_spmd.sunk | while | flops 17605632 | bytes 115360056 | solution.py:87
  (325 shorter events, 188.7 us)
Async XLA Ops:
  1.7 7.7 %copy-start.8 = (f32[2,64,8,256]{3,2,1,0:T(8,128)S(1)}, f32[2,64,8,256]{3,2,1,0:T(8,128)}, u32[]{:S(2)}) copy-start(f32[2,64,8,256]{3,2,1,0:T(8,128)} %param.4) | copy-start | bytes 3145732
  2.8 19.2 %collective-permute-start = (f32[2,64,5,256]{3,1,2,0:T(8,128)}, f32[2,64,5,256]{3,1,2,0:T(8,128)}, u32[]{:S(2)}, u32[]{:S(2)}) collective-permute-start(f32[2,64,5,256]{3,1,2,0:T(8,128)} %copy.102), channel_id=1, source_target_pairs={{0,1},{1,2},{2,3},{3,4},{4,5},{5,6},{6,7},{7,8},{8,9},{9,10},{10,1... | collective-permute-start | bytes 1966088 | tf_op jit(solution)/shard_map/ppermute | solution.py:18
  4.7 6.2 %copy-start.39 = (s32[128,8]{0,1:T(8,128)S(1)}, s32[128,8]{0,1:T(8,128)}, u32[]{:S(2)}) copy-start(s32[128,8]{0,1:T(8,128)} %param.5) | copy-start | bytes 12292
  5.8 19.9 %collective-permute-start.1 = (f32[2,64,5,256]{3,1,2,0:T(8,128)}, f32[2,64,5,256]{3,1,2,0:T(8,128)}, u32[]{:S(2)}, u32[]{:S(2)}) collective-permute-start(f32[2,64,5,256]{3,1,2,0:T(8,128)} %copy.103), channel_id=1, source_target_pairs={{1,0},{2,1},{3,2},{4,3},{5,4},{6,5},{7,6},{8,7},{9,8},{10,9},{11,1... | collective-permute-start | bytes 1966088 | tf_op jit(solution)/shard_map/ppermute | solution.py:20
  41.2 27.4 %all-to-all-start = ((f32[2,1,294912]{2,1,0:T(1,128)}), f32[2,1,294912]{2,1,0:T(1,128)S(1)}, u32[]{:S(2)}, u32[]{:S(2)}) async-start(f32[2,1,294912]{2,1,0:T(1,128)} %reshape.70), calls=%async_computation | async-start | bytes 4718592 | tf_op jit(solution)/shard_map/all_to_all | solution.py:91
  99.4 9.1 %collective-permute-start.2 = (f32[2,128,18,5]{1,0,3,2:T(2,128)S(1)}, f32[2,128,18,5]{1,0,3,2:T(2,128)S(1)}, u32[]{:S(2)}, u32[]{:S(2)}) collective-permute-start(f32[2,128,18,5]{1,0,3,2:T(2,128)S(1)} %copy.77), channel_id=1, source_target_pairs={{0,16},{1,17},{2,18},{3,19},{4,20},{5,21},{6,22},{7,23},{8,24},{9,... | collective-permute-start | bytes 276488 | tf_op jit(solution)/shard_map/ppermute | solution.py:18
  104.0 6.4 %collective-permute-start.3 = (f32[2,128,18,5]{1,0,3,2:T(2,128)S(1)}, f32[2,128,18,5]{1,0,3,2:T(2,128)S(1)}, u32[]{:S(2)}, u32[]{:S(2)}) collective-permute-start(f32[2,128,18,5]{1,0,3,2:T(2,128)S(1)} %copy.78), channel_id=1, source_target_pairs={{16,0},{17,1},{18,2},{19,3},{20,4},{21,5},{22,6},{23,7},{24,8},{25... | collective-permute-start | bytes 276488 | tf_op jit(solution)/shard_map/ppermute | solution.py:20
  176.0 6.2 %copy-start.16 = (f32[1,128,18,138]{1,0,3,2:T(1,128)S(1)}, f32[1,128,18,138]{1,0,3,2:T(1,128)}, u32[]{:S(2)}) copy-start(f32[1,128,18,138]{1,0,3,2:T(1,128)} %fusion.59) | copy-start | bytes 3815428
  182.9 2.3 copy-start.29
  182.9 2.3 copy-start.30
  194.3 7.0 %copy-start.28 = (f32[1,123,18,138]{1,0,3,2:T(1,128)S(1)}, f32[1,123,18,138]{1,0,3,2:T(1,128)}, u32[]{:S(2)}) copy-start(f32[1,123,18,138]{1,0,3,2:T(1,128)} %get-tuple-element.203) | copy-start | bytes 3666388
  217.1 1.9 copy-start.26
  234.3 1.9 copy-start.24
  251.5 1.9 copy-start.22
  269.2 1.9 copy-start.20
  286.6 1.9 copy-start.18
  302.8 2.6 copy-start.15
  302.8 2.6 copy-start.37
  310.9 2.3 copy-start.10
  310.9 2.4 copy-start.32
  316.1 2.3 copy-start.9
  316.1 2.4 copy-start.31
  324.4 1.9 copy-start.4
  327.6 1.9 copy-start.2
  341.6 1.9 copy-start.4
  344.7 1.9 copy-start.2
  358.7 1.9 copy-start.4
  361.9 1.9 copy-start.2
  375.8 1.9 copy-start.4
  379.0 1.9 copy-start.2
  393.0 1.9 copy-start.4
  396.1 1.9 copy-start.2
  (41 other events, 58.2 us)
where the time goes:
time: 416 us; the launch traced here: 409 us
  other arithmetic  154 us (37%)
  local copies, waits for them, and re-layouts  145 us (35%)
  matrix products  58.9 us (14%)
  waiting for transfers between devices  36 us (9%)
  starting transfers between devices  13.6 us (3%)
    another operation x8, local copies, waits for them, and re-layouts, coherence(): sums = box_sum(jnp.stack([prod_re, prod_im]))  51.5 us
    add x8, other arithmetic, coherence(): prod_re = earlier[0] * later[0] + earlier[1] * later[1]  50.5 us
    dot_general x9, matrix products, box_sum(): jnp.einsum('...rc,kr->...kc', samples, row_table, precision=lax.Precision...  48.7 us
    sub x40, other arithmetic, apply_matrix(): back_im = coh_re * vector[1] - coh_im * vector[0]  39 us
    unnamed x71, local copies, waits for them, and re-layouts  27.1 us
    all_to_all x1, waiting for transfers between devices, regroup(): lax.all_to_all(samples, 'date', split_axis=3, concat_axis=1, tiled=True)  23 us
    another operation x8, other arithmetic, coherence(): sums = box_sum(jnp.stack([prod_re, prod_im]))  22.7 us
    reduce_sum x5, other arithmetic, apply_matrix(): meansq = jnp.mean(image[0] * image[0] + image[1] * image[1], axis=0)  20.3 us
  transfers between devices with their start and end apart: 5, of which 3 were waited for; matrix products, arithmetic and copies ran while one was open for 3% of the time, Pallas kernels for 0%

commit v1 on v0

--- a/solution.py
+++ b/solution.py
@@ -1,3 +1,4 @@
+import functools
 import jax
 import jax.numpy as jnp
 from jax import lax
@@ -5,6 +6,21 @@
 
 LOOK = 5
 ITERS = 5
+
+
+def mix_stops_all_over_axis(w_in, axis_name):
+    return jnp.concatenate(
+        lax.all_to_all(
+            jnp.stack(jnp.split(w_in, lax.axis_size(axis_name), 3), axis=0),
+            axis_name=axis_name,
+            split_axis=0,
+            concat_axis=0,
+        ),
+        1,
+    )
+
+
+replace_run = functools.partial(mix_stops_all_over_axis, axis_name="date")
 
 
 def extended_2(cells, sides, width):
@@ -88,7 +104,7 @@
 
 
 def regroup(samples):
-    return lax.all_to_all(samples, "date", split_axis=3, concat_axis=1, tiled=True)
+    return replace_run(samples)
 
 
 def add_row_rims(samples):

time: 416 us -> 376 us (0.904)
  local copies, waits for them, and re-layouts: 145 us -> 115 us
  other arithmetic: 154 us -> 141 us
    unnamed x71 -> x70, local copies, waits for them, and re-layouts: 27.1 us -> 11.4 us
    all_to_all x4 -> x1, local copies, waits for them, and re-layouts: 12 us -> 1.82 us  [mix_stops_all_over_axis(): lax.all_to_all(jnp.stack(jnp.split(w_in, lax.axis_size(axis_name), 3), ax...]
    all_to_all x1 -> x0, other arithmetic: 9.05 us -> none  [regroup(): lax.all_to_all(samples, 'date', split_axis=3, concat_axis=1, tiled=True)]
    ppermute x2 -> x0, local copies, waits for them, and re-layouts: 7.13 us -> none  [the longest x1 3.6 us: extended_2(): lax.ppermute(tail, axis, [(i, (i + 1) % count) for i in range(ends)])]
    unnamed x1 -> x0, other arithmetic: 6.05 us -> none
  transfers between devices with their start and end apart: 5 -> 5, of which waited for: 3 -> 3; matrix products, arithmetic and copies ran while one was open for 3% -> 2% of each run, Pallas kernels for 0% -> 0%
where the time goes in v1:
time: 376 us; the launch traced here: 371 us
  other arithmetic  141 us (38%)
  local copies, waits for them, and re-layouts  115 us (31%)
  matrix products  58.9 us (16%)
  waiting for transfers between devices  40.1 us (11%)
  starting transfers between devices  14.7 us (4%)
    another operation x8, local copies, waits for them, and re-layouts, coherence(): sums = box_sum(jnp.stack([prod_re, prod_im]))  51.4 us
    add x8, other arithmetic, coherence(): prod_re = earlier[0] * later[0] + earlier[1] * later[1]  50.4 us
    dot_general x9, matrix products, box_sum(): jnp.einsum('...rc,kr->...kc', samples, row_table, precision=lax.Precision...  48.7 us
    sub x40, other arithmetic, apply_matrix(): back_im = coh_re * vector[1] - coh_im * vector[0]  38.8 us
    all_to_all x1, waiting for transfers between devices, mix_stops_all_over_axis(): lax.all_to_all(jnp.stack(jnp.split(w_in, lax.axis_size(axis_name), 3), ax...  25.5 us
    another operation x8, other arithmetic, coherence(): sums = box_sum(jnp.stack([prod_re, prod_im]))  22.7 us
    reduce_sum x5, other arithmetic, apply_matrix(): meansq = jnp.mean(image[0] * image[0] + image[1] * image[1], axis=0)  20.3 us
    while x70, local copies, waits for them, and re-layouts  19.5 us
  transfers between devices with their start and end apart: 5, of which 3 were waited for; matrix products, arithmetic and copies ran while one was open for 2% of the time, Pallas kernels for 0%

profile of v1, /device:TPU:10, one launch (start us, length us, event | category | flops | bytes accessed | tf_op | source)
XLA Modules:
  0.0 371.2 jit_solution(7460842613589673557)
XLA Ops:
  7.9 13.1 %collective-permute-done = f32[2,64,5,256]{3,1,2,0:T(8,128)S(1)} collective-permute-done((f32[2,64,5,256]{3,1,2,0:T(8,128)S(1)}, f32[2,64,5,256]{3,1,2,0:T(8,128)S(1)}, u32[]{:S(2)}, u32[]{:S(2)}) %collective-permute-start) | collective-permute-done | bytes 655392 | tf_op jit(solution)/shard_map/ppermute | solution.py:34
  23.3 4.9 %all-to-all-start = ((f32[2,2,64,18,128]{4,2,3,1,0:T(8,128)}), f32[2,2,64,18,128]{4,2,3,1,0:T(8,128)}, u32[]{:S(2)}, u32[]{:S(2)}) async-start(f32[2,2,64,18,128]{4,2,3,1,0:T(8,128)} %pad_maximum_fusion.9), calls=%async_computation | async-start | bytes 4718592 | tf_op jit(solution)/shard_map/all_to_all | solution.py:13
  28.3 25.5 %all-to-all-done = f32[2,2,64,18,128]{4,2,3,1,0:T(8,128)} async-done(((f32[2,2,64,18,128]{4,2,3,1,0:T(8,128)}), f32[2,2,64,18,128]{4,2,3,1,0:T(8,128)}, u32[]{:S(2)}, u32[]{:S(2)}) %all-to-all-start) | async-done | bytes 2359328 | tf_op jit(solution)/shard_map/all_to_all | solution.py:13
  74.8 5.5 %multiply_add_fusion.9 = (f32[1,121,18,138]{1,0,3,2:T(1,128)S(1)}, f32[1,121,18,138]{1,0,3,2:T(1,128)S(1)}) fusion(f32[2,128,18,138]{1,0,3,2:T(2,128)S(1)} %pad_maximum_fusion), kind=kLoop, calls=%fused_computation.114 | loop fusion | flops 1803384 | bytes 7213536 | tf_op jit(solution)/shard_map/add | solution.py:68
  83.0 6.4 %multiply_add_fusion.8 = (f32[1,120,18,138]{1,0,3,2:T(1,128)}, f32[1,120,18,138]{1,0,3,2:T(1,128)}) fusion(f32[2,128,18,138]{1,0,3,2:T(2,128)S(1)} %pad_maximum_fusion), kind=kLoop, calls=%fused_computation.112 | loop fusion | flops 1788480 | bytes 7153920 | tf_op jit(solution)/shard_map/add | solution.py:68
  89.4 6.3 %multiply_add_fusion.11 = (f32[1,123,18,138]{1,0,3,2:T(1,128)}, f32[1,123,18,138]{1,0,3,2:T(1,128)}) fusion(f32[2,128,18,138]{1,0,3,2:T(2,128)S(1)} %pad_maximum_fusion), kind=kLoop, calls=%fused_computation.118 | loop fusion | flops 1833192 | bytes 7332768 | tf_op jit(solution)/shard_map/add | solution.py:68
  95.7 6.4 %multiply_add_fusion.10 = (f32[1,122,18,138]{1,0,3,2:T(1,128)}, f32[1,122,18,138]{1,0,3,2:T(1,128)}) fusion(f32[2,128,18,138]{1,0,3,2:T(2,128)S(1)} %pad_maximum_fusion), kind=kLoop, calls=%fused_computation.116 | loop fusion | flops 1818288 | bytes 7273152 | tf_op jit(solution)/shard_map/add | solution.py:68
  102.1 6.6 %multiply_add_fusion.13 = (f32[1,125,18,138]{1,0,3,2:T(1,128)}, f32[1,125,18,138]{1,0,3,2:T(1,128)}) fusion(f32[2,128,18,138]{1,0,3,2:T(2,128)S(1)} %pad_maximum_fusion), kind=kLoop, calls=%fused_computation.122 | loop fusion | flops 1863000 | bytes 7452000 | tf_op jit(solution)/shard_map/add | solution.py:68
  108.7 6.4 %multiply_add_fusion.12 = (f32[1,124,18,138]{1,0,3,2:T(1,128)}, f32[1,124,18,138]{1,0,3,2:T(1,128)}) fusion(f32[2,128,18,138]{1,0,3,2:T(2,128)S(1)} %pad_maximum_fusion), kind=kLoop, calls=%fused_computation.120 | loop fusion | flops 1848096 | bytes 7392384 | tf_op jit(solution)/shard_map/add | solution.py:68
  115.0 6.5 %multiply_add_fusion.15 = (f32[1,127,18,138]{1,0,3,2:T(1,128)}, f32[1,127,18,138]{1,0,3,2:T(1,128)}) fusion(f32[2,128,18,138]{1,0,3,2:T(2,128)S(1)} %pad_maximum_fusion), kind=kLoop, calls=%fused_computation.126 | loop fusion | flops 1892808 | bytes 7571232 | tf_op jit(solution)/shard_map/add | solution.py:68
  121.5 6.4 %multiply_add_fusion.14 = (f32[1,126,18,138]{1,0,3,2:T(1,128)}, f32[1,126,18,138]{1,0,3,2:T(1,128)}) fusion(f32[2,128,18,138]{1,0,3,2:T(2,128)S(1)} %pad_maximum_fusion), kind=kLoop, calls=%fused_computation.124 | loop fusion | flops 1877904 | bytes 7511616 | tf_op jit(solution)/shard_map/add | solution.py:68
  130.7 6.5 %copy.63 = f32[2,121,18,138]{3,2,1,0:T(8,128)} copy(f32[2,121,18,138]{1,0,3,2:T(2,128)S(1)} %pad_maximum_fusion.7) | data formatting | bytes 4809024 | tf_op jit(solution)/shard_map/stack | solution.py:70
  137.2 6.2 %fusion.91 = f32[8,2,121,138]{3,0,2,1:T(8,128)} fusion(f32[2,121,18,138]{3,2,1,0:T(8,128)} %copy.63), kind=kOutput, calls=%fused_computation.179 | convolution fusion | flops 57708864 | bytes 3473184 | tf_op jit(solution)/shard_map/...rc,kr->...kc/dot_general | solution.py:56
  149.3 6.5 %copy.65 = f32[2,120,18,138]{3,2,1,0:T(8,128)} copy(f32[2,120,18,138]{1,0,3,2:T(2,128)S(1)} %pad_maximum_fusion.8) | data formatting | bytes 4769280 | tf_op jit(solution)/shard_map/stack | solution.py:70
  155.8 6.1 %fusion.89 = f32[8,2,120,138]{3,0,2,1:T(8,128)} fusion(f32[2,120,18,138]{3,2,1,0:T(8,128)} %copy.65), kind=kOutput, calls=%fused_computation.177 | convolution fusion | flops 57231936 | bytes 3444480 | tf_op jit(solution)/shard_map/...rc,kr->...kc/dot_general | solution.py:56
  166.2 6.3 %copy.59 = f32[2,123,18,138]{3,2,1,0:T(8,128)} copy(f32[2,123,18,138]{1,0,3,2:T(2,128)S(1)} %pad_maximum_fusion.5) | data formatting | bytes 4888512 | tf_op jit(solution)/shard_map/stack | solution.py:70
  172.5 6.1 %fusion.95 = f32[8,2,123,138]{3,0,2,1:T(8,128)} fusion(f32[2,123,18,138]{3,2,1,0:T(8,128)} %copy.59), kind=kOutput, calls=%fused_computation.183 | convolution fusion | flops 58662720 | bytes 3530592 | tf_op jit(solution)/shard_map/...rc,kr->...kc/dot_general | solution.py:56
  183.3 6.4 %copy.61 = f32[2,122,18,138]{3,2,1,0:T(8,128)} copy(f32[2,122,18,138]{1,0,3,2:T(2,128)S(1)} %pad_maximum_fusion.6) | data formatting | bytes 4848768 | tf_op jit(solution)/shard_map/stack | solution.py:70
  189.7 6.0 %fusion.93 = f32[8,2,122,138]{3,0,2,1:T(8,128)} fusion(f32[2,122,18,138]{3,2,1,0:T(8,128)} %copy.61), kind=kOutput, calls=%fused_computation.181 | convolution fusion | flops 58185792 | bytes 3501888 | tf_op jit(solution)/shard_map/...rc,kr->...kc/dot_general | solution.py:56
  200.4 6.3 %copy.55 = f32[2,125,18,138]{3,2,1,0:T(8,128)} copy(f32[2,125,18,138]{1,0,3,2:T(2,128)S(1)} %pad_maximum_fusion.3) | data formatting | bytes 4968000 | tf_op jit(solution)/shard_map/stack | solution.py:70
  206.7 6.2 %fusion.99 = f32[8,2,125,138]{3,0,2,1:T(8,128)} fusion(f32[2,125,18,138]{3,2,1,0:T(8,128)} %copy.55), kind=kOutput, calls=%fused_computation.187 | convolution fusion | flops 59616576 | bytes 3588000 | tf_op jit(solution)/shard_map/...rc,kr->...kc/dot_general | solution.py:56
  217.6 6.7 %copy.57 = f32[2,124,18,138]{3,2,1,0:T(8,128)} copy(f32[2,124,18,138]{1,0,3,2:T(2,128)S(1)} %pad_maximum_fusion.4) | data formatting | bytes 4928256 | tf_op jit(solution)/shard_map/stack | solution.py:70
  224.3 6.2 %fusion.97 = f32[8,2,124,138]{3,0,2,1:T(8,128)} fusion(f32[2,124,18,138]{3,2,1,0:T(8,128)} %copy.57), kind=kOutput, calls=%fused_computation.185 | convolution fusion | flops 59139648 | bytes 3559296 | tf_op jit(solution)/shard_map/...rc,kr->...kc/dot_general | solution.py:56
  235.2 6.3 %copy.49 = f32[2,127,18,138]{3,2,1,0:T(8,128)} copy(f32[2,127,18,138]{1,0,3,2:T(2,128)S(1)} %pad_maximum_fusion.1) | data formatting | bytes 5047488 | tf_op jit(solution)/shard_map/stack | solution.py:70
  241.5 6.3 %fusion.103 = f32[8,2,127,138]{3,0,2,1:T(8,128)} fusion(f32[2,127,18,138]{3,2,1,0:T(8,128)} %copy.49), kind=kOutput, calls=%fused_computation.191 | convolution fusion | flops 60570432 | bytes 3645408 | tf_op jit(solution)/shard_map/...rc,kr->...kc/dot_general | solution.py:56
  252.6 6.5 %copy.53 = f32[2,126,18,138]{3,2,1,0:T(8,128)} copy(f32[2,126,18,138]{1,0,3,2:T(2,128)S(1)} %pad_maximum_fusion.2) | data formatting | bytes 5007744 | tf_op jit(solution)/shard_map/stack | solution.py:70
  259.1 4.9 %fusion.101 = f32[8,2,126,138]{3,0,2,1:T(8,128)S(1)} fusion(f32[2,126,18,138]{3,2,1,0:T(8,128)} %copy.53), kind=kOutput, calls=%fused_computation.189 | convolution fusion | flops 60093504 | bytes 3616704 | tf_op jit(solution)/shard_map/...rc,kr->...kc/dot_general | solution.py:56
  284.4 85.6 %while.12 = (s32[]{:T(128)}, f32[2,128,8,128]{3,2,1,0:T(8,128)S(1)}, f32[1,2,128,8,128]{4,3,2,1,0:T(8,128)}, f32[1,2,128,8,128]{4,3,2,1,0:T(8,128)}, f32[1,2,128...) while((s32[]{:T(128)}, ...), condition=%wide.region_2.3_spmd, body=%wide.region_0.2_spmd.sunk | while | flops 17605632 | bytes 115360056 | solution.py:103
  314.5 4.1 %add_reduce_fusion.2 = (f32[8,128]{1,0:T(8,128)S(1)}, f32[128,8,128]{2,1,0:T(8,128)S(1)}, f32[128,8,128]{2,1,0:T(8,128)S(1)}) fusion(f32[120,8,128]{2,1,0:T(8,128)} %get-tuple-element.328, f32[1,2,128,8,128]{4,3,2,1,0:T(8,128)S(1)} %get-tuple-element.392, f32[2,120,8,128]{3,2,1,0:T(8,128)S(1)} %slice.1368, f32[121,8,128]{2,1,0:T(8,128)} %get-tuple-element.331, ...), kind=kLoop, calls=%fused_computation.33.clone.1 | loop fusion | flops 11009024 | bytes 26677248 | tf_op jit(solution)/shard_map/while/body/eval_jaxpr/reduce_sum | solution.py:93
  331.6 4.1 %add_reduce_fusion.2 = (f32[8,128]{1,0:T(8,128)S(1)}, f32[128,8,128]{2,1,0:T(8,128)S(1)}, f32[128,8,128]{2,1,0:T(8,128)S(1)}) fusion(f32[120,8,128]{2,1,0:T(8,128)} %get-tuple-element.328, f32[1,2,128,8,128]{4,3,2,1,0:T(8,128)S(1)} %get-tuple-element.392, f32[2,120,8,128]{3,2,1,0:T(8,128)S(1)} %slice.1368, f32[121,8,128]{2,1,0:T(8,128)} %get-tuple-element.331, ...), kind=kLoop, calls=%fused_computation.33.clone.1 | loop fusion | flops 11009024 | bytes 26677248 | tf_op jit(solution)/shard_map/while/body/eval_jaxpr/reduce_sum | solution.py:93
  348.7 4.1 %add_reduce_fusion.2 = (f32[8,128]{1,0:T(8,128)S(1)}, f32[128,8,128]{2,1,0:T(8,128)S(1)}, f32[128,8,128]{2,1,0:T(8,128)S(1)}) fusion(f32[120,8,128]{2,1,0:T(8,128)} %get-tuple-element.328, f32[1,2,128,8,128]{4,3,2,1,0:T(8,128)S(1)} %get-tuple-element.392, f32[2,120,8,128]{3,2,1,0:T(8,128)S(1)} %slice.1368, f32[121,8,128]{2,1,0:T(8,128)} %get-tuple-element.331, ...), kind=kLoop, calls=%fused_computation.33.clone.1 | loop fusion | flops 11009024 | bytes 26677248 | tf_op jit(solution)/shard_map/while/body/eval_jaxpr/reduce_sum | solution.py:93
  365.8 4.1 %add_reduce_fusion.2 = (f32[8,128]{1,0:T(8,128)S(1)}, f32[128,8,128]{2,1,0:T(8,128)S(1)}, f32[128,8,128]{2,1,0:T(8,128)S(1)}) fusion(f32[120,8,128]{2,1,0:T(8,128)} %get-tuple-element.328, f32[1,2,128,8,128]{4,3,2,1,0:T(8,128)S(1)} %get-tuple-element.392, f32[2,120,8,128]{3,2,1,0:T(8,128)S(1)} %slice.1368, f32[121,8,128]{2,1,0:T(8,128)} %get-tuple-element.331, ...), kind=kLoop, calls=%fused_computation.33.clone.1 | loop fusion | flops 11009024 | bytes 26677248 | tf_op jit(solution)/shard_map/while/body/eval_jaxpr/reduce_sum | solution.py:93
  (321 shorter events, 160.0 us)
Async XLA Ops:
  1.7 6.1 %copy-start.39 = (s32[128,8]{0,1:T(8,128)S(1)}, s32[128,8]{0,1:T(8,128)}, u32[]{:S(2)}) copy-start(s32[128,8]{0,1:T(8,128)} %param.5) | copy-start | bytes 12292
  1.7 19.3 %copy-start.8 = (f32[2,64,8,256]{3,2,1,0:T(8,128)S(1)}, f32[2,64,8,256]{3,2,1,0:T(8,128)}, u32[]{:S(2)}) copy-start(f32[2,64,8,256]{3,2,1,0:T(8,128)} %param.4) | copy-start | bytes 3145732
  1.9 19.1 %collective-permute-start = (f32[2,64,5,256]{3,1,2,0:T(8,128)S(1)}, f32[2,64,5,256]{3,1,2,0:T(8,128)S(1)}, u32[]{:S(2)}, u32[]{:S(2)}) collective-permute-start(f32[2,64,5,256]{3,1,2,0:T(8,128)S(1)} %copy.79), channel_id=1, source_target_pairs={{0,1},{1,2},{2,3},{3,4},{4,5},{5,6},{6,7},{7,8},{8,9},{9,10},{10,1... | collective-permute-start | bytes 1966088 | tf_op jit(solution)/shard_map/ppermute | solution.py:34
  4.2 17.2 %collective-permute-start.1 = (f32[2,64,5,256]{3,1,2,0:T(8,128)S(1)}, f32[2,64,5,256]{3,1,2,0:T(8,128)S(1)}, u32[]{:S(2)}, u32[]{:S(2)}) collective-permute-start(f32[2,64,5,256]{3,1,2,0:T(8,128)S(1)} %copy.80), channel_id=1, source_target_pairs={{1,0},{2,1},{3,2},{4,3},{5,4},{6,5},{7,6},{8,7},{9,8},{10,9},{11,1... | collective-permute-start | bytes 1966088 | tf_op jit(solution)/shard_map/ppermute | solution.py:36
  23.3 30.5 %all-to-all-start = ((f32[2,2,64,18,128]{4,2,3,1,0:T(8,128)}), f32[2,2,64,18,128]{4,2,3,1,0:T(8,128)}, u32[]{:S(2)}, u32[]{:S(2)}) async-start(f32[2,2,64,18,128]{4,2,3,1,0:T(8,128)} %pad_maximum_fusion.9), calls=%async_computation | async-start | bytes 4718592 | tf_op jit(solution)/shard_map/all_to_all | solution.py:13
  61.0 9.5 %collective-permute-start.2 = (f32[2,128,18,5]{1,0,3,2:T(2,128)S(1)}, f32[2,128,18,5]{1,0,3,2:T(2,128)S(1)}, u32[]{:S(2)}, u32[]{:S(2)}) collective-permute-start(f32[2,128,18,5]{1,0,3,2:T(2,128)S(1)} %copy.46), channel_id=1, source_target_pairs={{0,16},{1,17},{2,18},{3,19},{4,20},{5,21},{6,22},{7,23},{8,24},{9,... | collective-permute-start | bytes 276488 | tf_op jit(solution)/shard_map/ppermute | solution.py:34
  65.6 6.4 %collective-permute-start.3 = (f32[2,128,18,5]{1,0,3,2:T(2,128)S(1)}, f32[2,128,18,5]{1,0,3,2:T(2,128)S(1)}, u32[]{:S(2)}, u32[]{:S(2)}) collective-permute-start(f32[2,128,18,5]{1,0,3,2:T(2,128)S(1)} %copy.47), channel_id=1, source_target_pairs={{16,0},{17,1},{18,2},{19,3},{20,4},{21,5},{22,6},{23,7},{24,8},{25... | collective-permute-start | bytes 276488 | tf_op jit(solution)/shard_map/ppermute | solution.py:36
  137.2 6.2 %copy-start.16 = (f32[1,128,18,138]{1,0,3,2:T(1,128)S(1)}, f32[1,128,18,138]{1,0,3,2:T(1,128)}, u32[]{:S(2)}) copy-start(f32[1,128,18,138]{1,0,3,2:T(1,128)} %fusion.59) | copy-start | bytes 3815428
  144.1 2.3 copy-start.29
  144.1 2.3 copy-start.30
  155.8 7.0 %copy-start.28 = (f32[1,123,18,138]{1,0,3,2:T(1,128)S(1)}, f32[1,123,18,138]{1,0,3,2:T(1,128)}, u32[]{:S(2)}) copy-start(f32[1,123,18,138]{1,0,3,2:T(1,128)} %get-tuple-element.203) | copy-start | bytes 3666388
  178.6 1.9 copy-start.26
  195.7 1.9 copy-start.24
  212.9 1.9 copy-start.22
  230.5 1.9 copy-start.20
  247.9 1.9 copy-start.18
  270.0 1.6 copy-start.35
  272.7 2.3 copy-start.10
  272.7 2.4 copy-start.32
  275.1 1.6 copy-start.33
  277.9 2.3 copy-start.9
  277.9 2.4 copy-start.31
  286.2 1.9 copy-start.4
  289.4 1.9 copy-start.2
  303.3 1.9 copy-start.4
  306.5 1.9 copy-start.2
  320.5 1.9 copy-start.4
  323.6 1.9 copy-start.2
  337.6 1.9 copy-start.4
  340.7 1.9 copy-start.2
  354.7 1.9 copy-start.4
  357.8 1.9 copy-start.2
  (41 other events, 58.1 us)
